TPU v7x, 32 devices: a whole 2x2x4 slice. The times are simulated.
32 devices in a mesh: seq: 8 (over z, y), head: 4 (over x, core).
Axes of the slice: x: 2, y: 2, z: 4, core: 2. Of those that a mesh axis runs over, the one named last changes fastest.
Arguments:
- tokens: bfloat16 [1024, 2048], P('seq'), may hold values from -20 to 20, as said below
- projection: bfloat16 [2048, 3072], P(None, 'head'), may hold values from -0.078125 to 0.078125
- context_cotangent: bfloat16 [1024, 2048], P('seq', 'head'), may hold values from -80 to 80
Outputs:
- perturbed_context: bfloat16 [1024, 2048], P('seq', 'head')
- ascent_direction: float32 [2048, 3072], P('seq', 'head')
Inputs may be any that keep to these rules, and one draw needn't show every extreme that they name: `tokens`: activations of the layer.
All inputs are finite; a program needn't handle non-finite values.
Results may differ from a plain program's by a relative error of at most 0.017.
Values may be sent and summed in bfloat16 or wider, within the bound.
A program may use at most 64 MiB of HBM per device.

v0:
```python
import math

import jax
import jax.numpy as jnp
from jax import lax
from jax.sharding import PartitionSpec as P

INPUT_FEATURES = 2048
KEY_VALUE_HEADS = 4
HEAD_DIMENSION = 128
QUERY_PER_GROUP = 4


masked_score = -1e30
key_block = 512


def attend_fold(query_rows, query_pos, score_scale):
    head_size = query_rows.shape[1]

    def single_block(carry_state, block_rows, offset):
        running_max, row_total, context_sum = carry_state
        key_rows = block_rows[:, :head_size]
        value_rows = block_rows[:, head_size:].astype(jnp.float32)
        scores = jnp.dot(query_rows, key_rows.T, preferred_element_type=jnp.float32) * score_scale
        key_pos = offset + jnp.arange(block_rows.shape[0], dtype=jnp.int32)
        allowed = key_pos[None, :] <= query_pos[:, None]
        scores = jnp.where(allowed, scores, masked_score)
        new_max = jnp.maximum(running_max, jnp.max(scores, axis=1))
        factor = jnp.exp(running_max - new_max)
        weights = jnp.where(allowed, jnp.exp(scores - new_max[:, None]), 0.0)
        row_total = row_total * factor + jnp.sum(weights, axis=1)
        context_sum = context_sum * factor[:, None] + jnp.dot(
            weights, value_rows, precision=lax.Precision.HIGHEST, preferred_element_type=jnp.float32
        )
        return (new_max, row_total, context_sum)

    def fold_keys(carry_state, block_rows, offset):
        row_count = block_rows.shape[0]
        if row_count > key_block and row_count % key_block == 0:

            def sub_block(block_index, inner_state):
                part_rows = lax.dynamic_slice_in_dim(
                    block_rows, block_index * key_block, key_block, 0
                )
                return single_block(inner_state, part_rows, block_index * key_block)

            return lax.fori_loop(0, row_count // key_block, sub_block, carry_state)
        return single_block(carry_state, block_rows, offset)

    return fold_keys


def on_device(tokens, projection, context_cotangent):
    score_scale = HEAD_DIMENSION ** (-0.5)
    local_rows = tokens.shape[0]
    rows_all = local_rows * QUERY_PER_GROUP
    first_row = lax.axis_index("seq") * local_rows
    query_pos = first_row + jnp.arange(rows_all, dtype=jnp.int32) // QUERY_PER_GROUP

    def split_heads(projected_weight):
        reshaped_grads = projected_weight.reshape(local_rows, QUERY_PER_GROUP + 2, HEAD_DIMENSION)
        query_rows = reshaped_grads[:, :QUERY_PER_GROUP].reshape(rows_all, HEAD_DIMENSION)
        key_value = reshaped_grads[:, QUERY_PER_GROUP:].reshape(local_rows, 2 * HEAD_DIMENSION)
        return (query_rows, key_value)

    def empty_state():
        return (
            jnp.full((rows_all,), masked_score, jnp.float32),
            jnp.zeros((rows_all,), jnp.float32),
            jnp.zeros((rows_all, HEAD_DIMENSION), jnp.float32),
        )

    projected_weight = jnp.dot(tokens, projection, preferred_element_type=jnp.float32).astype(
        jnp.bfloat16
    )
    query_rows, key_value = split_heads(projected_weight)
    gathered = lax.all_gather(key_value, "seq", axis=0, tiled=True)
    total_rows = gathered.shape[0]
    block_size = min(key_block, total_rows)
    needed = (first_row + local_rows - 1) // block_size + 1
    fold_first = attend_fold(query_rows, query_pos, score_scale)

    def forward_step(block_index, carry_state):
        block_rows = lax.dynamic_slice_in_dim(gathered, block_index * block_size, block_size, 0)
        return fold_first(carry_state, block_rows, block_index * block_size)

    running_max, row_total, context_sum = lax.fori_loop(0, needed, forward_step, empty_state())
    context = (context_sum / row_total[:, None]).astype(jnp.bfloat16)
    log_total = running_max + jnp.log(row_total)
    grad_rows = context_cotangent.reshape(rows_all, HEAD_DIMENSION)
    row_delta = jnp.sum(grad_rows.astype(jnp.float32) * context.astype(jnp.float32), axis=1)
    contract_rows = (((0,), (0,)), ((), ()))

    def backward_step(block_index, carry_state):
        query_grad, key_terms = carry_state
        offset = block_index * block_size
        block_rows = lax.dynamic_slice_in_dim(gathered, offset, block_size, 0)
        key_rows = block_rows[:, :HEAD_DIMENSION]
        value_rows = block_rows[:, HEAD_DIMENSION:]
        scores = jnp.dot(query_rows, key_rows.T, preferred_element_type=jnp.float32) * score_scale
        key_pos = offset + jnp.arange(block_size, dtype=jnp.int32)
        allowed = key_pos[None, :] <= query_pos[:, None]
        probs_full = jnp.where(allowed, jnp.exp(scores - log_total[:, None]), 0.0)
        probs_half = probs_full.astype(jnp.bfloat16)
        prob_grad = jnp.dot(grad_rows, value_rows.T, preferred_element_type=jnp.float32)
        score_grad = (probs_full * (prob_grad - row_delta[:, None]) * score_scale).astype(
            jnp.bfloat16
        )
        query_grad = query_grad + jnp.dot(score_grad, key_rows, preferred_element_type=jnp.float32)
        key_grad = lax.dot_general(
            score_grad, query_rows, contract_rows, preferred_element_type=jnp.float32
        )
        value_grad = lax.dot_general(
            probs_half, grad_rows, contract_rows, preferred_element_type=jnp.float32
        )
        key_terms = lax.dynamic_update_slice_in_dim(
            key_terms, jnp.concatenate([key_grad, value_grad], axis=1), offset, 0
        )
        return (query_grad, key_terms)

    initial = (
        jnp.zeros((rows_all, HEAD_DIMENSION), jnp.float32),
        jnp.zeros((total_rows, 2 * HEAD_DIMENSION), jnp.float32),
    )
    query_grad, key_terms = lax.fori_loop(0, needed, backward_step, initial)
    key_value_grad = lax.psum_scatter(key_terms, "seq", scatter_dimension=0, tiled=True).astype(
        jnp.bfloat16
    )
    head_grads = jnp.concatenate(
        [
            query_grad.astype(jnp.bfloat16).reshape(local_rows, QUERY_PER_GROUP * HEAD_DIMENSION),
            key_value_grad,
        ],
        axis=1,
    )
    grad_term = lax.dot_general(
        tokens, head_grads, contract_rows, preferred_element_type=jnp.float32
    )
    normalizing_scale = math.sqrt(
        INPUT_FEATURES * KEY_VALUE_HEADS * (QUERY_PER_GROUP + 2) * HEAD_DIMENSION
    )
    ascent_radius = 0.2 * math.sqrt(KEY_VALUE_HEADS * (QUERY_PER_GROUP + 2) * HEAD_DIMENSION)
    weight_grad = lax.psum(grad_term, "seq")
    square_sum = lax.psum(jnp.sum(weight_grad * weight_grad), "head")
    grad_norm = jnp.sqrt(square_sum)
    share_rows = INPUT_FEATURES // lax.axis_size("seq")
    own_grad = lax.dynamic_slice_in_dim(
        weight_grad, lax.axis_index("seq") * share_rows, share_rows, 0
    )
    direction = own_grad * (normalizing_scale / grad_norm)
    moved_weights = (
        projection.astype(jnp.float32) + ascent_radius / grad_norm * weight_grad
    ).astype(jnp.bfloat16)
    projected_new = jnp.dot(tokens, moved_weights, preferred_element_type=jnp.float32).astype(
        jnp.bfloat16
    )
    query_new, key_value_new = split_heads(projected_new)
    fold_new = attend_fold(query_new, query_pos, score_scale)
    final_state = fold_new(
        empty_state(), lax.all_gather(key_value_new, "seq", axis=0, tiled=True), jnp.int32(0)
    )
    perturbed = (
        (final_state[2] / final_state[1][:, None])
        .astype(jnp.bfloat16)
        .reshape(local_rows, QUERY_PER_GROUP * HEAD_DIMENSION)
    )
    return (perturbed, direction)


def solution(mesh):
    return jax.shard_map(
        on_device,
        mesh=mesh,
        in_specs=(P("seq", None), P(None, "head"), P("seq", "head")),
        out_specs=(P("seq", "head"), P("seq", "head")),
        check_vma=False,
    )
```

profile of v0, /device:TPU:0, one launch (start us, length us, event | category | flops | bytes accessed | tf_op | source)
XLA Modules:
  0.0 397.3 jit_solution(14726550498906386122)
XLA Ops:
  7.2 0.0 reduce-scatter.2.cloned.1.call-start
  7.2 1.0 copy-done
  8.2 2.5 convolution_convert_fusion
  10.7 0.2 copy.21
  10.9 0.1 copy.22
  11.0 33.0 %all_gather.6 = bf16[1024,256]{1,0:T(8,128)(2,1)S(1)} all-gather(bf16[128,256]{1,0:T(8,128)(2,1)S(1)} %copy.22), channel_id=1, replica_groups=mesh['seq'=8,'head'=4] {'seq'}, dimensions={0}, use_global_device_ids=true | all-gather | bytes 589824 | tf_op jit(solution)/shard_map/all_gather | solution.py:78
  44.0 0.1 copy.23
  44.2 1.8 while.46
  44.3 0.3 fusion.107
  44.6 0.2 fusion.108
  44.9 1.2 convolution_add_fusion.6
  46.1 0.1 reshape.57
  46.2 0.2 multiply_reduce_fusion.1
  46.4 1.1 broadcast_in_dim.50
  47.6 2.6 while.47
  47.6 0.4 fusion.120
  48.0 0.3 fusion.121
  48.3 0.3 fusion.123
  48.6 0.3 fusion.122
  48.9 0.9 maximum_dynamic-update-slice_fusion.2
  49.8 0.4 convolution_add_fusion.7
  50.1 0.0 reduce-scatter.2.cloned.1.call-update
  50.2 0.0 all-reduce.2.cloned.1.call-start
  50.2 0.1 reshape.58
  50.3 70.2 %reduce-scatter.2.cloned.1.call-done = f32[128,256]{0,1:T(8,128)} async-done(((f32[1024,256]{0,1:T(8,128)}), f32[128,256]{0,1:T(8,128)}) %reduce-scatter.2.cloned.1.call-update) | async-done | bytes 131088 | tf_op jit(solution)/shard_map/reduce_scatter | solution.py:127
  120.6 0.9 convert_element_type.49
  121.5 0.1 copy.24
  121.6 3.7 convolution_bitcast_fusion
  125.3 0.0 all-reduce.2.cloned.1.call-update
  125.3 4.7 %copy.20 = bf16[2048,768]{0,1:T(8,128)(2,1)} copy(bf16[2048,768]{1,0:T(8,128)(2,1)} %param.10) | data formatting | bytes 6291456 | tf_op args[1]
  130.0 204.6 %all-reduce.2.cloned.1.call-done = f32[2048,768]{0,1:T(8,128)} async-done(((f32[2048,768]{0,1:T(8,128)}), f32[2048,768]{0,1:T(8,128)}) %all-reduce.2.cloned.1.call-update) | async-done | bytes 6291472 | tf_op jit(solution)/shard_map/psum | solution.py:144
  334.6 5.0 %multiply_reduce_fusion = f32[]{:T(128)} fusion(f32[2048,768]{0,1:T(8,128)} %all-reduce.2.cloned.1.call-done), kind=kLoop, calls=%fused_computation.85 | loop fusion | flops 3145727 | bytes 6291460 | tf_op jit(solution)/shard_map/reduce_sum | solution.py:145
  339.6 6.8 %psum.15 = f32[]{:T(128)} all-reduce(f32[]{:T(128)} %multiply_reduce_fusion), channel_id=1, replica_groups=mesh['seq'=8,'head'=4] {'head'}, use_global_device_ids=true, to_apply=%region_10.11 | all-reduce | flops 1 | bytes 8 | tf_op jit(solution)/shard_map/psum | solution.py:145
  347.2 4.7 %fusion.58 = bf16[768,128]{1,0:T(8,128)(2,1)S(1)} fusion(bf16[128,2048]{1,0:T(8,128)(2,1)S(1)} %copy-done, f32[2048,768]{0,1:T(8,128)} %all-reduce.2.cloned.1.call-done, bf16[2048,768]{0,1:T(8,128)(2,1)} %copy.20, f32[]{:T(128)S(6)} %div.45), kind=kOutput, calls=%fused_computation.89 | convolution fusion | flops 409042944 | bytes 10158084 | tf_op jit(solution)/shard_map/dot_general | solution.py:155
  352.0 1.2 dynamic-slice_multiply_fusion
  353.2 1.1 copy.27
  354.3 0.1 copy.28
  354.4 31.3 %all_gather.7 = bf16[1024,256]{1,0:T(8,128)(2,1)S(1)} all-gather(bf16[128,256]{1,0:T(8,128)(2,1)S(1)} %copy.28), channel_id=1, replica_groups=mesh['seq'=8,'head'=4] {'seq'}, dimensions={0}, use_global_device_ids=true | all-gather | bytes 589824 | tf_op jit(solution)/shard_map/all_gather | solution.py:161
  385.8 0.1 copy.26
  385.9 3.6 while.48
  385.9 0.3 fusion.127
  386.3 0.2 fusion.128
  386.5 1.2 convolution_add_fusion.8
  387.7 0.3 fusion.127
  388.1 0.2 fusion.128
  388.3 1.2 convolution_add_fusion.8
  389.5 0.1 divide_convert_fusion
  389.7 0.7 reshape.62
  (29 shorter events, 0.2 us)
Async XLA Ops:
  7.2 1.0 copy-start
  7.2 113.4 %reduce-scatter.2.cloned.1.call-start = ((), (), s32[]{:S(2)}) async-start(), calls=%async_computation.1 | async-start | bytes 1179648 | tf_op jit(solution)/shard_map/reduce_scatter | solution.py:127
  44.2 1.8 copy-start.1
  50.2 284.5 %all-reduce.2.cloned.1.call-start = ((), (), s32[]{:S(2)}) async-start(), calls=%async_computation.2 | async-start | bytes 12582912 | tf_op jit(solution)/shard_map/psum | solution.py:144
Sparse Core Ops, SparseCore 0:
  50.3 70.2 reduce-scatter.1
  125.4 209.1 all-reduce.1
where the time goes:
time: 398 us; the launch traced here: 397 us
  waiting for transfers between devices  275 us (69%)
  blocking collectives  71.2 us (18%)
  matrix products  16.9 us (4%)
  between operations  15 us (4%)
  local copies, waits for them, and re-layouts  9.76 us (2%)
  other arithmetic  9.18 us (2%)
    psum x1, waiting for transfers between devices, on_device(): weight_grad = lax.psum(grad_term, 'seq')  205 us
    reduce_scatter x1, waiting for transfers between devices, on_device(): lax.psum_scatter(key_terms, 'seq', scatter_dimension=0, tiled=True)  70.2 us
    all_gather x1, blocking collectives, on_device(): gathered = lax.all_gather(key_value, 'seq', axis=0, tiled=True)  33 us
    all_gather x1, blocking collectives, on_device(): lax.all_gather(key_value_new, 'seq', axis=0, tiled=True)  31.3 us
  transfers between devices with their start and end apart: 2, of which 2 were waited for; matrix products, arithmetic and copies ran while one was open for 1% of the time, Pallas kernels for 0%

commit v1 on v0

--- a/solution.py
+++ b/solution.py
@@ -1,8 +1,11 @@
+import functools
 import math
 
 import jax
 import jax.numpy as jnp
 from jax import lax
+from jax.experimental import pallas as pl
+from jax.experimental.pallas import tpu as pltpu
 from jax.sharding import PartitionSpec as P
 
 INPUT_FEATURES = 2048
@@ -168,9 +171,341 @@
     return (perturbed, direction)
 
 
+def exchange_kernel(seq_size, tokens_ref, cotangent_ref, tokens_out, cotangent_out, *sems):
+    (local_sem, own_sent, own_sent_c, fold_sent, fold_sent_c, got, got_c,
+     across_sent, pair_sent, relay_sent, across_got, pair_got, relay_got) = sems
+    s = lax.axis_index("seq")
+    h = lax.axis_index("head")
+    rows_here = tokens_ref.shape[0]
+    parts = tokens_out.shape[0]
+    width = tokens_out.shape[2]
+
+    def flip(index, mask):
+        bit = 1
+        while bit <= mask:
+            if mask & bit:
+                index = index + bit - 2 * bit * ((index // bit) % 2)
+            bit *= 2
+        return index
+
+    def rows(index):
+        return pl.ds(pl.multiple_of(index * rows_here, rows_here), rows_here)
+
+    def columns(index):
+        return pl.ds(pl.multiple_of(index * width, width), width)
+
+    def remote(source, target, send, receive, mask_s, mask_h):
+        return pltpu.make_async_remote_copy(
+            src_ref=source, dst_ref=target, send_sem=send, recv_sem=receive,
+            device_id=(flip(s, mask_s), flip(h, mask_h)), device_id_type=pl.DeviceIdType.MESH,
+        )
+
+    even = [k for k in range(2, seq_size, 2)]
+    direct = [1] + even
+    barrier = pltpu.get_barrier_semaphore()
+    greeted = [(k, 0) for k in direct] + [(0, 1), (0, 2)]
+    for mask_s, mask_h in greeted:
+        pl.semaphore_signal(barrier, inc=1, device_id=(flip(s, mask_s), flip(h, mask_h)),
+                            device_id_type=pl.DeviceIdType.MESH)
+    pl.semaphore_wait(barrier, len(greeted))
+
+    own_tokens = tokens_ref.at[:, columns(h)]
+    own_place = tokens_out.at[h, rows(s)]
+    own_place_c = cotangent_out.at[rows(s)]
+    sent = []
+    for k in even + [1]:
+        copy = remote(own_tokens, own_place, own_sent.at[k], got.at[k], k, 0)
+        copy.start()
+        sent.append(copy)
+    for k in even + [1]:
+        copy = remote(cotangent_ref, own_place_c, own_sent_c.at[k], got_c.at[k], k, 0)
+        copy.start()
+        sent.append(copy)
+    local = [pltpu.make_async_copy(tokens_ref.at[:, columns(q)], tokens_out.at[q, rows(s)],
+                                   local_sem.at[q]) for q in range(parts)]
+    local.append(pltpu.make_async_copy(cotangent_ref, own_place_c, local_sem.at[parts]))
+    for copy in local:
+        copy.start()
+
+    def arrived(k):
+        place = tokens_out.at[h, rows(flip(s, k))]
+        remote(place, place, own_sent.at[0], got.at[k], 1, 0).wait_recv()
+        if k % 2 == 0:
+            copy = remote(place, place, fold_sent.at[k], got.at[k + 1], 1, 0)
+            copy.start()
+            sent.append(copy)
+        for semaphores, mask in (((across_sent, across_got), 2), ((pair_sent, pair_got), 1)):
+            copy = remote(place, place, semaphores[0].at[k], semaphores[1].at[k], 0, mask)
+            copy.start()
+            sent.append(copy)
+
+    def arrived_c(k):
+        place = cotangent_out.at[rows(flip(s, k))]
+        remote(place, place, own_sent.at[0], got_c.at[k], 1, 0).wait_recv()
+        if k % 2 == 0:
+            copy = remote(place, place, fold_sent_c.at[k], got_c.at[k + 1], 1, 0)
+            copy.start()
+            sent.append(copy)
+
+    def relay(k):
+        place = tokens_out.at[flip(h, 2), rows(flip(s, k))]
+        remote(place, place, own_sent.at[0], across_got.at[k], 0, 2).wait_recv()
+        copy = remote(place, place, relay_sent.at[k], relay_got.at[k], 0, 1)
+        copy.start()
+        sent.append(copy)
+
+    order = [even[0], 1] + even[1:] + [k + 1 for k in even]
+    for position, k in enumerate(order):
+        arrived(k)
+        if k % 2 == 0:
+            arrived_c(k)
+        if position >= 2:
+            relay(order[position - 2])
+    for k in order[-2:]:
+        relay(k)
+    for k in order:
+        if k % 2:
+            arrived_c(k)
+    for k in order:
+        place = tokens_out.at[flip(h, 1), rows(flip(s, k))]
+        remote(place, place, own_sent.at[0], pair_got.at[k], 0, 1).wait_recv()
+        place = tokens_out.at[flip(h, 3), rows(flip(s, k))]
+        remote(place, place, own_sent.at[0], relay_got.at[k], 0, 1).wait_recv()
+    for copy in sent:
+        copy.wait_send()
+    for copy in local:
+        copy.wait()
+
+
+def exchange(tokens, cotangent, seq_size, parts):
+    local_rows, features = tokens.shape
+    total = local_rows * seq_size
+    return pl.pallas_call(
+        functools.partial(exchange_kernel, seq_size),
+        out_shape=(
+            jax.ShapeDtypeStruct((parts, total, features // parts), tokens.dtype),
+            jax.ShapeDtypeStruct((total, cotangent.shape[1]), cotangent.dtype),
+        ),
+        in_specs=[pl.BlockSpec(memory_space=pltpu.VMEM)] * 2,
+        out_specs=(pl.BlockSpec(memory_space=pltpu.VMEM),) * 2,
+        scratch_shapes=[pltpu.SemaphoreType.DMA((parts + 1,))]
+        + [pltpu.SemaphoreType.DMA((seq_size,))] * 12,
+        compiler_params=pltpu.CompilerParams(collective_id=0, has_side_effects=True),
+        name="exchange",
+    )(tokens, cotangent)
+
+
+CONTRACT_LAST = (((1,), (1,)), ((), ()))
+CONTRACT_FIRST = (((0,), (0,)), ((), ()))
+SCALE = HEAD_DIMENSION ** (-0.5)
+SCALE_LOG2 = SCALE * math.log2(math.e)
+QW = QUERY_PER_GROUP * HEAD_DIMENSION
+D = HEAD_DIMENSION
+
+
+def gradient_kernel(
+    tokens, projection, cotangent, own_grad, squares, base_q, base_kv, move_q, move_kv,
+    projected, base, key_t, value_t, grads, key_sum, value_sum, weight_half,
+):
+    s = lax.axis_index("seq")
+    parts, total, width = tokens.shape
+    tile = min(256, total)
+    local_rows = base_q.shape[0]
+    share = own_grad.shape[0]
+
+    def token_rows(rows, weights, columns):
+        acc = jnp.dot(tokens[0, rows, :], weights[pl.ds(0, width), columns],
+                      preferred_element_type=jnp.float32)
+        for q in range(1, parts):
+            acc += jnp.dot(tokens[q, rows, :], weights[pl.ds(q * width, width), columns],
+                           preferred_element_type=jnp.float32)
+        return acc
+
+    @pl.loop(0, total // tile)
+    def _(block):
+        rows = pl.ds(pl.multiple_of(block * tile, tile), tile)
+        acc = token_rows(rows, projection, slice(None))
+        base[rows, :] = acc
+        half = acc.astype(jnp.bfloat16)
+        projected[rows, :] = half
+        half_f = half.astype(jnp.float32)
+        key_t[:, rows] = half_f[:, QW : QW + D].T.astype(jnp.bfloat16)
+        value_t[:, rows] = half_f[:, QW + D :].T.astype(jnp.bfloat16)
+
+    own_rows = pl.ds(pl.multiple_of(s * local_rows, local_rows), local_rows)
+    base_q[...] = base[own_rows, :QW]
+    base_kv[...] = base[:, QW:]
+    key_sum[...] = jnp.zeros_like(key_sum)
+    value_sum[...] = jnp.zeros_like(value_sum)
+
+    allowed = lax.broadcasted_iota(jnp.int32, (tile, tile), 0) <= lax.broadcasted_iota(
+        jnp.int32, (tile, tile), 1
+    )
+    for block in range(total // tile):
+        length = (block + 1) * tile
+        rows = slice(block * tile, length)
+
+        @pl.loop(0, QUERY_PER_GROUP)
+        def _(head):
+            columns = pl.ds(pl.multiple_of(head * D, D), D)
+            query = projected[rows, columns]
+            out_grad = cotangent[rows, columns]
+            scores = lax.dot_general(projected[:length, QW : QW + D], query, CONTRACT_LAST,
+                                     preferred_element_type=jnp.float32)
+            last = jnp.where(allowed, scores[block * tile :], masked_score)
+            scores = last if block == 0 else jnp.concatenate([scores[: block * tile], last], 0)
+            top = jnp.max(scores, axis=0, keepdims=True)
+            weights = jnp.exp2(scores * SCALE_LOG2 - top * SCALE_LOG2)
+            probs = weights * (1.0 / jnp.sum(weights, axis=0, keepdims=True))
+            probs_half = probs.astype(jnp.bfloat16)
+            context_t = jnp.dot(value_t[:, :length], probs_half,
+                                preferred_element_type=jnp.float32)
+            context_t = context_t.astype(jnp.bfloat16).astype(jnp.float32)
+            delta = jnp.sum(out_grad.astype(jnp.float32).T * context_t, axis=0, keepdims=True)
+            prob_grad = lax.dot_general(projected[:length, QW + D :], out_grad, CONTRACT_LAST,
+                                        preferred_element_type=jnp.float32)
+            score_grad = (probs * (prob_grad - delta)).astype(jnp.bfloat16)
+            query_t = jnp.dot(key_t[:, :length], score_grad, preferred_element_type=jnp.float32)
+            grads[rows, columns] = (query_t * SCALE).T.astype(jnp.bfloat16)
+            key_sum[:length, :] += jnp.dot(score_grad, query, preferred_element_type=jnp.float32)
+            value_sum[:length, :] += jnp.dot(probs_half, out_grad,
+                                             preferred_element_type=jnp.float32)
+
+    grads[:, QW : QW + D] = (key_sum[...] * SCALE).astype(jnp.bfloat16)
+    grads[:, QW + D :] = value_sum[...].astype(jnp.bfloat16)
+
+    squares[...] = jnp.zeros_like(squares)
+    per_part = width // share
+
+    @pl.loop(0, parts * per_part)
+    def _(chunk):
+        columns = pl.ds(pl.multiple_of((chunk % per_part) * share, share), share)
+        rows = pl.ds(pl.multiple_of(chunk * share, share), share)
+        block = lax.dot_general(tokens[chunk // per_part, :, columns], grads[...], CONTRACT_FIRST,
+                                preferred_element_type=jnp.float32)
+        squares[...] += jnp.sum(block * block, axis=0, keepdims=True)
+        weight_half[rows, :] = block.astype(jnp.bfloat16)
+
+        @pl.when(chunk == s)
+        def _():
+            own_grad[...] = block
+
+    move_q[...] = token_rows(own_rows, weight_half, slice(0, QW))
+
+    @pl.loop(0, total // tile)
+    def _(block):
+        rows = pl.ds(pl.multiple_of(block * tile, tile), tile)
+        move_kv[rows, :] = token_rows(rows, weight_half, slice(QW, None))
+
+
+def gradients(tokens_all, projection, cotangent_all, local_rows, share):
+    parts, total, width = tokens_all.shape
+    features, columns = projection.shape
+    f32, bf16 = jnp.float32, jnp.bfloat16
+    shape = jax.ShapeDtypeStruct
+    return pl.pallas_call(
+        gradient_kernel,
+        out_shape=(
+            shape((share, columns), f32),
+            shape((1, columns), f32),
+            shape((local_rows, QW), f32),
+            shape((total, 2 * D), f32),
+            shape((local_rows, QW), f32),
+            shape((total, 2 * D), f32),
+        ),
+        in_specs=[pl.BlockSpec(memory_space=pltpu.VMEM)] * 3,
+        out_specs=(pl.BlockSpec(memory_space=pltpu.VMEM),) * 6,
+        scratch_shapes=[
+            pltpu.VMEM((total, columns), bf16),
+            pltpu.VMEM((total, columns), f32),
+            pltpu.VMEM((D, total), bf16),
+            pltpu.VMEM((D, total), bf16),
+            pltpu.VMEM((total, columns), bf16),
+            pltpu.VMEM((total, D), f32),
+            pltpu.VMEM((total, D), f32),
+            pltpu.VMEM((features, columns), bf16),
+        ],
+        compiler_params=pltpu.CompilerParams(vmem_limit_bytes=VMEM_BUDGET),
+        name="gradients",
+    )(tokens_all, projection, cotangent_all)
+
+
+def perturbed_kernel(radius, root, norm_ref, own_grad, base_q, base_kv, move_q, move_kv, out,
+                     direction):
+    s = lax.axis_index("seq")
+    inverse = 1.0 / norm_ref[...]
+    direction[...] = own_grad[...] * (root * inverse)
+    step = radius * inverse
+    local_rows = base_q.shape[0]
+    total = base_kv.shape[0]
+    query = (base_q[...] + step * move_q[...]).astype(jnp.bfloat16)
+    key_value = (base_kv[...] + step * move_kv[...]).astype(jnp.bfloat16)
+    value_t = key_value[:, D:].astype(jnp.float32).T.astype(jnp.bfloat16)
+    stacked = jnp.concatenate(
+        [query[:, g * D : (g + 1) * D] for g in range(QUERY_PER_GROUP)], axis=0
+    )
+    scores = lax.dot_general(key_value[:, :D], stacked, CONTRACT_LAST,
+                             preferred_element_type=jnp.float32)
+    key_pos = lax.broadcasted_iota(jnp.int32, (total, local_rows), 0)
+    row_pos = lax.broadcasted_iota(jnp.int32, (total, local_rows), 1) + s * local_rows
+    allowed = key_pos <= row_pos
+    for g in range(QUERY_PER_GROUP):
+        part = jnp.where(allowed, scores[:, g * local_rows : (g + 1) * local_rows], masked_score)
+        top = jnp.max(part, axis=0, keepdims=True)
+        weights = jnp.exp2(part * SCALE_LOG2 - top * SCALE_LOG2)
+        sums = jnp.sum(weights, axis=0, keepdims=True)
+        context_t = jnp.dot(value_t, weights.astype(jnp.bfloat16),
+                            preferred_element_type=jnp.float32) / sums
+        out[:, g * D : (g + 1) * D] = context_t.T.astype(jnp.bfloat16)
+
+
+VMEM_BUDGET = 60 * 1024 * 1024
+
+
+def resident_step(tokens, projection, context_cotangent):
+    seq_size, head_size = lax.axis_size("seq"), lax.axis_size("head")
+    local_rows, features = tokens.shape
+    columns = projection.shape[1]
+    share = features // seq_size
+    tokens_all, cotangent_all = exchange(tokens, context_cotangent, seq_size, head_size)
+    own_grad, squares, base_q, base_kv, move_q, move_kv = gradients(
+        tokens_all, projection, cotangent_all, local_rows, share
+    )
+    grad_norm = jnp.sqrt(lax.psum(jnp.sum(squares), "head")).reshape(1, 1)
+    root = math.sqrt(features * head_size * columns)
+    radius = 0.2 * math.sqrt(head_size * columns)
+    return pl.pallas_call(
+        functools.partial(perturbed_kernel, radius, root),
+        out_shape=(
+            jax.ShapeDtypeStruct((local_rows, QW), jnp.bfloat16),
+            jax.ShapeDtypeStruct((share, columns), jnp.float32),
+        ),
+        in_specs=[pl.BlockSpec(memory_space=pltpu.VMEM)] * 6,
+        out_specs=(pl.BlockSpec(memory_space=pltpu.VMEM),) * 2,
+        compiler_params=pltpu.CompilerParams(vmem_limit_bytes=VMEM_BUDGET),
+        name="perturbed",
+    )(grad_norm, own_grad, base_q, base_kv, move_q, move_kv)
+
+
+def fits(local_rows, features, columns, seq_size, head_size):
+    total = local_rows * seq_size
+    share = features // seq_size
+    held = total * (2 * features + 2 * QW + 12 * columns + 24 * D) + 4 * features * columns
+    pairs = seq_size >= 4 and seq_size & (seq_size - 1) == 0 and head_size == 4
+    aligned = share % 128 == 0 and (features // head_size) % share == 0 and local_rows % 128 == 0
+    return pairs and aligned and held < VMEM_BUDGET // 2
+
+
+def step(tokens, projection, context_cotangent):
+    sizes = (*tokens.shape, projection.shape[1], lax.axis_size("seq"), lax.axis_size("head"))
+    if fits(*sizes):
+        return resident_step(tokens, projection, context_cotangent)
+    return on_device(tokens, projection, context_cotangent)
+
+
 def solution(mesh):
     return jax.shard_map(
-        on_device,
+        step,
         mesh=mesh,
         in_specs=(P("seq", None), P(None, "head"), P("seq", "head")),
         out_specs=(P("seq", "head"), P("seq", "head")),

time: 398 us -> 93.6 us (0.24)
  waiting for transfers between devices: 275 us -> 0 us
  Pallas kernels: 0 us -> 83.9 us
  blocking collectives: 71.2 us -> 6.77 us
  matrix products: 16.9 us -> 0 us
  between operations: 15 us -> 1.33 us
  local copies, waits for them, and re-layouts: 9.76 us -> 0 us
  other arithmetic: 9.18 us -> 1.3 us
    psum x1 -> x0, waiting for transfers between devices: 205 us -> none  [on_device(): weight_grad = lax.psum(grad_term, 'seq')]
    pallas_call x0 -> x3, Pallas kernels: none -> 83.9 us  [the longest x1 43.8 us: exchange(): pl.pallas_call(functools.partial(exchange_kernel, seq_size), out_shape=(j...]
    reduce_scatter x1 -> x0, waiting for transfers between devices: 70.2 us -> none  [on_device(): lax.psum_scatter(key_terms, 'seq', scatter_dimension=0, tiled=True)]
    all_gather x2 -> x0, blocking collectives: 64.4 us -> none  [the longest x1 33 us: on_device(): gathered = lax.all_gather(key_value, 'seq', axis=0, tiled=True)]
    dot_general x14 -> x0, matrix products: 16.9 us -> none  [the longest x1 4.69 us: on_device(): jnp.dot(tokens, moved_weights, preferred_element_type=jnp.float32)]
    unnamed x6 -> x0, local copies, waits for them, and re-layouts: 6.88 us -> none
    reduce_sum x5 -> x1, other arithmetic: 5.96 us -> 1.3 us  [resident_step(): grad_norm = jnp.sqrt(lax.psum(jnp.sum(squares), 'head')).reshape(1, 1)]
  transfers between devices with their start and end apart: 2 -> 0, of which waited for: 2 -> 0; matrix products, arithmetic and copies ran while one was open for 1% -> 0% of each run, Pallas kernels for 0% -> 0%
where the time goes in v1:
time: 93.6 us; the launch traced here: 93.3 us
  Pallas kernels  83.9 us (90%)
  blocking collectives  6.77 us (7%)
  between operations  1.33 us (1%)
  other arithmetic  1.3 us (1%)
    pallas_call x1, Pallas kernels, exchange(): pl.pallas_call(functools.partial(exchange_kernel, seq_size), out_shape=(j...  43.8 us
    pallas_call x1, Pallas kernels, gradients(): pl.pallas_call(gradient_kernel, out_shape=(shape((share, columns), f32),...  35.9 us
    psum x1, blocking collectives, resident_step(): grad_norm = jnp.sqrt(lax.psum(jnp.sum(squares), 'head')).reshape(1, 1)  6.77 us
    pallas_call x1, Pallas kernels, resident_step(): pl.pallas_call(functools.partial(perturbed_kernel, radius, root), out_sha...  4.18 us

profile of v1, /device:TPU:0, one launch (start us, length us, event | category | flops | bytes accessed | tf_op | source)
XLA Modules:
  0.0 93.3 jit_solution(8136912926425463657)
XLA Ops:
  0.6 43.8 %exchange.1 = (bf16[4,1024,512]{2,1,0:T(8,128)(2,1)}, bf16[1024,512]{1,0:T(8,128)(2,1)}) custom-call(bf16[128,2048]{1,0:T(8,128)(2,1)} %tokens_ref.1, bf16[128,512]{1,0:T(8,128)(2,1)} %cotangent_ref.1), custom_call_target="tpu_custom_call" | custom-call | tf_op jit(solution)/shard_map/exchange/pallas_call | solution.py:283
  44.5 35.9 %gradients.1 = (f32[256,768]{1,0:T(8,128)}, f32[1,768]{1,0:T(1,128)}, f32[128,512]{1,0:T(8,128)}, f32[1024,256]{1,0:T(8,128)}, f32[128,512]{1,0:T(8,128)}, /*index=5*/f32[1024,256]{1,0:T(8,128)}) custom-call(bf16[4,1024,512]{2,1,0:T(8,128)(2,1)} %get-tuple-element.10.tokens, bf16[2048,768]{1,0:T(8,128)(2,1)} %projection.1, ...), custom_call_target="tpu_custom_call" | custom-call | tf_op jit(solution)/shard_map/gradients/pallas_call | solution.py:406
  80.4 1.3 %reduce_sum.9 = f32[]{:T(128)} reduce(f32[1,768]{1,0:T(1,128)} %get-tuple-element.12, f32[]{:T(128)} %constant.0.clone.1), dimensions={0,1}, to_apply=%region_0.0 | reduce | flops 767 | bytes 3080 | tf_op jit(solution)/shard_map/reduce_sum | solution.py:474
  81.7 6.8 %psum.7 = f32[]{:T(128)} all-reduce(f32[]{:T(128)} %reduce_sum.9), channel_id=1, replica_groups=mesh['seq'=8,'head'=4] {'head'}, use_global_device_ids=true, to_apply=%region_1.0 | all-reduce | flops 1 | bytes 8 | tf_op jit(solution)/shard_map/psum | solution.py:474
  89.2 4.2 %perturbed.1 = (bf16[128,512]{1,0:T(8,128)(2,1)}, f32[256,768]{1,0:T(8,128)}) custom-call(f32[1,1]{1,0:T(1,128)} %bitcast.norm_ref, f32[256,768]{1,0:T(8,128)} %get-tuple-element.13.own_grad, f32[128,512]{1,0:T(8,128)} %get-tuple-element.14.base_q, f32[1024,256]{1,0:T(8,128)} %get-tuple-element.15.base_kv, f32[128,512]{1,0:T(8,128)} %get-tuple-element.16.move_q, ...), custom_call_target="tpu_custom_call" | custom-call | tf_op jit(solution)/shard_map/perturbed/pallas_call | solution.py:477

commit v2 on v0

--- a/solution.py
+++ b/solution.py
@@ -1,8 +1,11 @@
+import functools
 import math
 
 import jax
 import jax.numpy as jnp
 from jax import lax
+from jax.experimental import pallas as pl
+from jax.experimental.pallas import tpu as pltpu
 from jax.sharding import PartitionSpec as P
 
 INPUT_FEATURES = 2048
@@ -168,9 +171,311 @@
     return (perturbed, direction)
 
 
+CONTRACT_LAST = (((1,), (1,)), ((), ()))
+CONTRACT_FIRST = (((0,), (0,)), ((), ()))
+SCALE = HEAD_DIMENSION ** (-0.5)
+SCALE_LOG2 = SCALE * math.log2(math.e)
+QW = QUERY_PER_GROUP * HEAD_DIMENSION
+D = HEAD_DIMENSION
+VMEM_BUDGET = 60 * 1024 * 1024
+
+
+def flip(index, mask):
+    bit = 1
+    while bit <= mask:
+        if mask & bit:
+            index = index + bit - 2 * bit * ((index // bit) % 2)
+        bit *= 2
+    return index
+
+
+def resident_kernel(
+    seq_size, radius, root, tokens_ref, cotangent_ref, projection_hbm, out, direction,
+    tokens, cotangent, projection, projected, base_q, base_kv, key_t, value_t, grads,
+    key_sum, value_sum, weight_half, own_grad, move_q, move_kv, norms,
+    local_sem, load_sem, own_sent, own_sent_c, fold_sent, fold_sent_c, got, got_c,
+    across_sent, pair_sent, relay_sent, across_got, pair_got, relay_got, norm_sent, norm_got,
+):
+    s = lax.axis_index("seq")
+    h = lax.axis_index("head")
+    local_rows = tokens_ref.shape[0]
+    parts, total, width = tokens.shape
+    tile = min(256, total)
+    share = own_grad.shape[0]
+
+    def rows_of(index):
+        return pl.ds(pl.multiple_of(index * local_rows, local_rows), local_rows)
+
+    def columns_of(index):
+        return pl.ds(pl.multiple_of(index * width, width), width)
+
+    def remote(source, target, send, receive, mask_s, mask_h):
+        return pltpu.make_async_remote_copy(
+            src_ref=source, dst_ref=target, send_sem=send, recv_sem=receive,
+            device_id=(flip(s, mask_s), flip(h, mask_h)), device_id_type=pl.DeviceIdType.MESH,
+        )
+
+    load = pltpu.make_async_copy(projection_hbm, projection, load_sem)
+    load.start()
+    even = [k for k in range(2, seq_size, 2)]
+    barrier = pltpu.get_barrier_semaphore()
+    greeted = [(k, 0) for k in [1] + even] + [(0, q) for q in range(1, parts)]
+    for mask_s, mask_h in greeted:
+        pl.semaphore_signal(barrier, inc=1, device_id=(flip(s, mask_s), flip(h, mask_h)),
+                            device_id_type=pl.DeviceIdType.MESH)
+    pl.semaphore_wait(barrier, len(greeted))
+
+    sent = []
+
+    def send(source, target, send_sem, receive, mask_s, mask_h):
+        copy = remote(source, target, send_sem, receive, mask_s, mask_h)
+        copy.start()
+        sent.append(copy)
+
+    own_rows = rows_of(s)
+    for k in even + [1]:
+        send(tokens_ref.at[:, columns_of(h)], tokens.at[h, own_rows], own_sent.at[k], got.at[k],
+             k, 0)
+    for k in even + [1]:
+        send(cotangent_ref, cotangent.at[own_rows], own_sent_c.at[k], got_c.at[k], k, 0)
+    local = [pltpu.make_async_copy(tokens_ref.at[:, columns_of(q)], tokens.at[q, own_rows],
+                                   local_sem.at[q]) for q in range(parts)]
+    local.append(pltpu.make_async_copy(cotangent_ref, cotangent.at[own_rows],
+                                       local_sem.at[parts]))
+    for copy in local:
+        copy.start()
+
+    def token_rows(rows, weights, columns):
+        acc = jnp.dot(tokens[0, rows, :], weights[pl.ds(0, width), columns],
+                      preferred_element_type=jnp.float32)
+        for q in range(1, parts):
+            acc += jnp.dot(tokens[q, rows, :], weights[pl.ds(q * width, width), columns],
+                           preferred_element_type=jnp.float32)
+        return acc
+
+    def project(k):
+        rows = rows_of(flip(s, k))
+        if k:
+            place = tokens.at[flip(h, 1), rows]
+            remote(place, place, own_sent.at[0], pair_got.at[k], 0, 1).wait_recv()
+            place = tokens.at[flip(h, 3), rows]
+            remote(place, place, own_sent.at[0], relay_got.at[k], 0, 1).wait_recv()
+        acc = token_rows(rows, projection, slice(None))
+        if k == 0:
+            base_q[...] = acc[:, :QW]
+        base_kv[rows, :] = acc[:, QW:]
+        half = acc.astype(jnp.bfloat16)
+        projected[rows, :] = half
+        half_f = half.astype(jnp.float32)
+        key_t[:, rows] = half_f[:, QW : QW + D].T.astype(jnp.bfloat16)
+        value_t[:, rows] = half_f[:, QW + D :].T.astype(jnp.bfloat16)
+
+    def arrived(k):
+        place = tokens.at[h, rows_of(flip(s, k))]
+        remote(place, place, own_sent.at[0], got.at[k], 1, 0).wait_recv()
+        if k % 2 == 0:
+            send(place, place, fold_sent.at[k], got.at[k + 1], 1, 0)
+        send(place, place, across_sent.at[k], across_got.at[k], 0, 2)
+        send(place, place, pair_sent.at[k], pair_got.at[k], 0, 1)
+
+    def arrived_c(k):
+        place = cotangent.at[rows_of(flip(s, k))]
+        remote(place, place, own_sent.at[0], got_c.at[k], 1, 0).wait_recv()
+        if k % 2 == 0:
+            send(place, place, fold_sent_c.at[k], got_c.at[k + 1], 1, 0)
+
+    def relay(k):
+        place = tokens.at[flip(h, 2), rows_of(flip(s, k))]
+        remote(place, place, own_sent.at[0], across_got.at[k], 0, 2).wait_recv()
+        send(place, place, relay_sent.at[k], relay_got.at[k], 0, 1)
+
+    for copy in local:
+        copy.wait()
+    load.wait()
+
+    order = [even[0], 1] + [k for j in even[1:] for k in (j, )] + [k + 1 for k in even]
+    project_queue = [0] + order
+    for position, k in enumerate(order):
+        arrived(k)
+        if position >= 1:
+            relay(order[position - 1])
+        if position == 1:
+            project(project_queue.pop(0))
+        if position >= 4:
+            project(project_queue.pop(0))
+    relay(order[-1])
+    for k in even:
+        arrived_c(k)
+        project(project_queue.pop(0))
+    while project_queue:
+        project(project_queue.pop(0))
+    for k in order:
+        if k % 2:
+            arrived_c(k)
+
+    key_sum[...] = jnp.zeros_like(key_sum)
+    value_sum[...] = jnp.zeros_like(value_sum)
+
+    allowed = lax.broadcasted_iota(jnp.int32, (tile, tile), 0) <= lax.broadcasted_iota(
+        jnp.int32, (tile, tile), 1
+    )
+    for block in range(total // tile):
+        length = (block + 1) * tile
+        rows = slice(block * tile, length)
+
+        @pl.loop(0, QUERY_PER_GROUP)
+        def _(head):
+            columns = pl.ds(pl.multiple_of(head * D, D), D)
+            query = projected[rows, columns]
+            out_grad = cotangent[rows, columns]
+            scores = lax.dot_general(projected[:length, QW : QW + D], query, CONTRACT_LAST,
+                                     preferred_element_type=jnp.float32)
+            last = jnp.where(allowed, scores[block * tile :], masked_score)
+            scores = last if block == 0 else jnp.concatenate([scores[: block * tile], last], 0)
+            top = jnp.max(scores, axis=0, keepdims=True)
+            weights = jnp.exp2(scores * SCALE_LOG2 - top * SCALE_LOG2)
+            probs = weights * (1.0 / jnp.sum(weights, axis=0, keepdims=True))
+            probs_half = probs.astype(jnp.bfloat16)
+            context_t = jnp.dot(value_t[:, :length], probs_half,
+                                preferred_element_type=jnp.float32)
+            context_t = context_t.astype(jnp.bfloat16).astype(jnp.float32)
+            delta = jnp.sum(out_grad.astype(jnp.float32).T * context_t, axis=0, keepdims=True)
+            prob_grad = lax.dot_general(projected[:length, QW + D :], out_grad, CONTRACT_LAST,
+                                        preferred_element_type=jnp.float32)
+            score_grad = (probs * (prob_grad - delta)).astype(jnp.bfloat16)
+            query_t = jnp.dot(key_t[:, :length], score_grad, preferred_element_type=jnp.float32)
+            grads[rows, columns] = (query_t * SCALE).T.astype(jnp.bfloat16)
+            key_sum[:length, :] += jnp.dot(score_grad, query, preferred_element_type=jnp.float32)
+            value_sum[:length, :] += jnp.dot(probs_half, out_grad,
+                                             preferred_element_type=jnp.float32)
+
+    grads[:, QW : QW + D] = (key_sum[...] * SCALE).astype(jnp.bfloat16)
+    grads[:, QW + D :] = value_sum[...].astype(jnp.bfloat16)
+
+    per_part = width // share
+    norms[0] = jnp.zeros_like(norms[0])
+
+    @pl.loop(0, parts * per_part)
+    def _(chunk):
+        columns = pl.ds(pl.multiple_of((chunk % per_part) * share, share), share)
+        rows = pl.ds(pl.multiple_of(chunk * share, share), share)
+        block = lax.dot_general(tokens[chunk // per_part, :, columns], grads[...], CONTRACT_FIRST,
+                                preferred_element_type=jnp.float32)
+        squared = block * block
+        lanes = squared[:, :128]
+        for start in range(128, squared.shape[1], 128):
+            lanes += squared[:, start : start + 128]
+        norms[0] += jnp.sum(lanes.reshape(share // 8, 8, 128), axis=0)
+        weight_half[rows, :] = block.astype(jnp.bfloat16)
+
+        @pl.when(chunk == s)
+        def _():
+            own_grad[...] = block
+
+    move_q[...] = token_rows(own_rows, weight_half, slice(0, QW))
+    for q in range(1, parts):
+        send(norms.at[0], norms.at[q], norm_sent.at[q], norm_got.at[q], 0, q)
+
+    @pl.loop(0, total // tile)
+    def _(block):
+        rows = pl.ds(pl.multiple_of(block * tile, tile), tile)
+        move_kv[rows, :] = token_rows(rows, weight_half, slice(QW, None))
+
+    for q in range(1, parts):
+        remote(norms.at[q], norms.at[q], norm_sent.at[0], norm_got.at[q], 0, q).wait_recv()
+    square_sum = jnp.sum(jnp.sum(norms[...], axis=0), keepdims=True)
+    inverse = 1.0 / jnp.sqrt(square_sum)
+    direction[...] = own_grad[...] * (root * inverse)
+    step_size = radius * inverse
+    query = (base_q[...] + step_size * move_q[...]).astype(jnp.bfloat16)
+    key_value = (base_kv[...] + step_size * move_kv[...]).astype(jnp.bfloat16)
+    new_value_t = key_value[:, D:].astype(jnp.float32).T.astype(jnp.bfloat16)
+    stacked = jnp.concatenate(
+        [query[:, g * D : (g + 1) * D] for g in range(QUERY_PER_GROUP)], axis=0
+    )
+    scores = lax.dot_general(key_value[:, :D], stacked, CONTRACT_LAST,
+                             preferred_element_type=jnp.float32)
+    key_pos = lax.broadcasted_iota(jnp.int32, (total, local_rows), 0)
+    row_pos = lax.broadcasted_iota(jnp.int32, (total, local_rows), 1) + s * local_rows
+    visible = key_pos <= row_pos
+    for g in range(QUERY_PER_GROUP):
+        part = jnp.where(visible, scores[:, g * local_rows : (g + 1) * local_rows], masked_score)
+        top = jnp.max(part, axis=0, keepdims=True)
+        weights = jnp.exp2(part * SCALE_LOG2 - top * SCALE_LOG2)
+        sums = jnp.sum(weights, axis=0, keepdims=True)
+        context_t = jnp.dot(new_value_t, weights.astype(jnp.bfloat16),
+                            preferred_element_type=jnp.float32) / sums
+        out[:, g * D : (g + 1) * D] = context_t.T.astype(jnp.bfloat16)
+    for copy in sent:
+        copy.wait_send()
+
+
+def resident_step(tokens, projection, cotangent):
+    seq_size, parts = lax.axis_size("seq"), lax.axis_size("head")
+    local_rows, features = tokens.shape
+    columns = projection.shape[1]
+    share = features // seq_size
+    total = local_rows * seq_size
+    f32, bf16 = jnp.float32, jnp.bfloat16
+    root = math.sqrt(features * parts * columns)
+    radius = 0.2 * math.sqrt(parts * columns)
+    in_vmem = pl.BlockSpec(memory_space=pltpu.VMEM)
+    return pl.pallas_call(
+        functools.partial(resident_kernel, seq_size, radius, root),
+        out_shape=(
+            jax.ShapeDtypeStruct((local_rows, QW), bf16),
+            jax.ShapeDtypeStruct((share, columns), f32),
+        ),
+        in_specs=[in_vmem, in_vmem, pl.BlockSpec(memory_space=pl.ANY)],
+        out_specs=(in_vmem, in_vmem),
+        scratch_shapes=[
+            pltpu.VMEM((parts, total, features // parts), bf16),
+            pltpu.VMEM((total, QW), bf16),
+            pltpu.VMEM((features, columns), bf16),
+            pltpu.VMEM((total, columns), bf16),
+            pltpu.VMEM((local_rows, QW), f32),
+            pltpu.VMEM((total, 2 * D), f32),
+            pltpu.VMEM((D, total), bf16),
+            pltpu.VMEM((D, total), bf16),
+            pltpu.VMEM((total, columns), bf16),
+            pltpu.VMEM((total, D), f32),
+            pltpu.VMEM((total, D), f32),
+            pltpu.VMEM((features, columns), bf16),
+            pltpu.VMEM((share, columns), f32),
+            pltpu.VMEM((local_rows, QW), f32),
+            pltpu.VMEM((total, 2 * D), f32),
+            pltpu.VMEM((parts, 8, 128), f32),
+            pltpu.SemaphoreType.DMA((parts + 1,)),
+            pltpu.SemaphoreType.DMA,
+        ]
+        + [pltpu.SemaphoreType.DMA((seq_size,))] * 12
+        + [pltpu.SemaphoreType.DMA((parts,))] * 2,
+        compiler_params=pltpu.CompilerParams(
+            collective_id=0, has_side_effects=True, vmem_limit_bytes=VMEM_BUDGET
+        ),
+        name="resident",
+    )(tokens, cotangent, projection)
+
+
+def fits(local_rows, features, columns, seq_size, head_size):
+    total = local_rows * seq_size
+    share = features // seq_size
+    held = total * (2 * features + 2 * QW + 12 * columns + 24 * D) + 4 * features * columns
+    pairs = seq_size >= 4 and seq_size & (seq_size - 1) == 0 and head_size == 4
+    aligned = share % 128 == 0 and (features // head_size) % share == 0 and local_rows % 128 == 0
+    return pairs and aligned and held < VMEM_BUDGET // 2
+
+
+def step(tokens, projection, context_cotangent):
+    sizes = (*tokens.shape, projection.shape[1], lax.axis_size("seq"), lax.axis_size("head"))
+    if fits(*sizes):
+        return resident_step(tokens, projection, context_cotangent)
+    return on_device(tokens, projection, context_cotangent)
+
+
 def solution(mesh):
     return jax.shard_map(
-        on_device,
+        step,
         mesh=mesh,
         in_specs=(P("seq", None), P(None, "head"), P("seq", "head")),
         out_specs=(P("seq", "head"), P("seq", "head")),

time: 398 us -> 79 us (0.20)
  waiting for transfers between devices: 275 us -> 0 us
  Pallas kernels: 0 us -> 74.6 us
  blocking collectives: 71.2 us -> 0 us
  matrix products: 16.9 us -> 0 us
  between operations: 15 us -> 0.64 us
  other arithmetic: 9.18 us -> 0 us
  local copies, waits for them, and re-layouts: 9.76 us -> 3.63 us
    psum x1 -> x0, waiting for transfers between devices: 205 us -> none  [on_device(): weight_grad = lax.psum(grad_term, 'seq')]
    pallas_call x0 -> x1, Pallas kernels: none -> 74.6 us  [resident_step(): pl.pallas_call(functools.partial(resident_kernel, seq_size, radius, root)...]
    reduce_scatter x1 -> x0, waiting for transfers between devices: 70.2 us -> none  [on_device(): lax.psum_scatter(key_terms, 'seq', scatter_dimension=0, tiled=True)]
    all_gather x2 -> x0, blocking collectives: 64.4 us -> none  [the longest x1 33 us: on_device(): gathered = lax.all_gather(key_value, 'seq', axis=0, tiled=True)]
    dot_general x14 -> x0, matrix products: 16.9 us -> none  [the longest x1 4.69 us: on_device(): jnp.dot(tokens, moved_weights, preferred_element_type=jnp.float32)]
    psum x1 -> x0, blocking collectives: 6.83 us -> none  [on_device(): square_sum = lax.psum(jnp.sum(weight_grad * weight_grad), 'head')]
    reduce_sum x5 -> x0, other arithmetic: 5.96 us -> none  [the longest x1 5.01 us: on_device(): square_sum = lax.psum(jnp.sum(weight_grad * weight_grad), 'head')]
  transfers between devices with their start and end apart: 2 -> 0, of which waited for: 2 -> 0; matrix products, arithmetic and copies ran while one was open for 1% -> 0% of each run, Pallas kernels for 0% -> 0%
where the time goes in v2:
time: 79 us; the launch traced here: 78.8 us
  Pallas kernels  74.6 us (94%)
  local copies, waits for them, and re-layouts  3.63 us (5%)
    pallas_call x1, Pallas kernels, resident_step(): pl.pallas_call(functools.partial(resident_kernel, seq_size, radius, root)...  74.6 us
    unnamed x2, local copies, waits for them, and re-layouts  3.63 us

profile of v2, /device:TPU:0, one launch (start us, length us, event | category | flops | bytes accessed | tf_op | source)
XLA Modules:
  0.0 78.8 jit_solution(7078051263596734313)
XLA Ops:
  0.6 74.6 %resident.1 = (bf16[128,512]{1,0:T(8,128)(2,1)}, f32[256,768]{1,0:T(8,128)}) custom-call(bf16[128,2048]{1,0:T(8,128)(2,1)} %tokens_ref.1, bf16[128,512]{1,0:T(8,128)(2,1)} %cotangent_ref.1, bf16[2048,768]{1,0:T(8,128)(2,1)} %projection_hbm.1), custom_call_target="tpu_custom_call" | custom-call | tf_op jit(solution)/shard_map/resident/pallas_call | solution.py:423
  75.2 1.6 %copy.7 = bf16[128,512]{1,0:T(8,128)(2,1)} copy(bf16[128,512]{1,0:T(8,128)(2,1)} %get-tuple-element.4) | data formatting | bytes 262144
  76.8 2.1 %copy.8 = f32[256,768]{1,0:T(8,128)} copy(f32[256,768]{1,0:T(8,128)} %get-tuple-element.5) | data formatting | bytes 1572864

commit v3 on v2

--- a/solution.py
+++ b/solution.py
@@ -193,8 +193,9 @@
     seq_size, radius, root, tokens_ref, cotangent_ref, projection_hbm, out, direction,
     tokens, cotangent, projection, projected, base_q, base_kv, key_t, value_t, grads,
     key_sum, value_sum, weight_half, own_grad, move_q, move_kv, norms,
-    local_sem, load_sem, own_sent, own_sent_c, fold_sent, fold_sent_c, got, got_c,
-    across_sent, pair_sent, relay_sent, across_got, pair_got, relay_got, norm_sent, norm_got,
+    local_sem, load_sem, own_sent, own_sent_c, line_sent, line_sent_c, fold_sent, fold_sent_c,
+    got, got_c, across_sent, pair_sent, relay_sent, across_got, pair_got, relay_got,
+    norm_sent, norm_got,
 ):
     s = lax.axis_index("seq")
     h = lax.axis_index("head")
@@ -209,35 +210,69 @@
     def columns_of(index):
         return pl.ds(pl.multiple_of(index * width, width), width)
 
-    def remote(source, target, send, receive, mask_s, mask_h):
+    mesh_type = pl.DeviceIdType.MESH
+    partner = flip(s, 1)
+    side = s % 2
+    place_on_line = s // 2
+    length_of_line = seq_size // 2
+    has_right = place_on_line < length_of_line - 1
+    has_left = place_on_line > 0
+
+    def remote(source, target, send, receive, to_s, to_h):
         return pltpu.make_async_remote_copy(
             src_ref=source, dst_ref=target, send_sem=send, recv_sem=receive,
-            device_id=(flip(s, mask_s), flip(h, mask_h)), device_id_type=pl.DeviceIdType.MESH,
-        )
+            device_id=(to_s, to_h), device_id_type=mesh_type,
+        )
+
+    def line_block(j):
+        near = jnp.minimum(place_on_line, length_of_line - 1 - place_on_line)
+        alternate = place_on_line - 1 - j // 2 if j % 2 == 0 else place_on_line + 1 + j // 2
+        beyond = jnp.where(place_on_line > near, length_of_line - 2 - j, j + 1)
+        return jnp.where(j < 2 * near, alternate, beyond)
 
     load = pltpu.make_async_copy(projection_hbm, projection, load_sem)
     load.start()
-    even = [k for k in range(2, seq_size, 2)]
     barrier = pltpu.get_barrier_semaphore()
-    greeted = [(k, 0) for k in [1] + even] + [(0, q) for q in range(1, parts)]
-    for mask_s, mask_h in greeted:
-        pl.semaphore_signal(barrier, inc=1, device_id=(flip(s, mask_s), flip(h, mask_h)),
-                            device_id_type=pl.DeviceIdType.MESH)
-    pl.semaphore_wait(barrier, len(greeted))
+
+    def greet(to_s, to_h):
+        pl.semaphore_signal(barrier, inc=1, device_id=(to_s, to_h), device_id_type=mesh_type)
+
+    greet(partner, h)
+    for q in range(1, parts):
+        greet(s, flip(h, q))
+
+    @pl.when(has_right)
+    def _():
+        greet(s + 2, h)
+
+    @pl.when(has_left)
+    def _():
+        greet(s - 2, h)
+
+    both_sides = jnp.minimum(place_on_line, 1) + jnp.minimum(length_of_line - 1 - place_on_line, 1)
+    pl.semaphore_wait(barrier, parts + both_sides)
 
     sent = []
 
-    def send(source, target, send_sem, receive, mask_s, mask_h):
-        copy = remote(source, target, send_sem, receive, mask_s, mask_h)
-        copy.start()
-        sent.append(copy)
+    def send(source, target, send_sem, receive, to_s, to_h, when=None):
+        copy = remote(source, target, send_sem, receive, to_s, to_h)
+        sent.append((copy, when))
+        if when is None:
+            copy.start()
+        else:
+
+            @pl.when(when)
+            def _():
+                copy.start()
 
     own_rows = rows_of(s)
-    for k in even + [1]:
-        send(tokens_ref.at[:, columns_of(h)], tokens.at[h, own_rows], own_sent.at[k], got.at[k],
-             k, 0)
-    for k in even + [1]:
-        send(cotangent_ref, cotangent.at[own_rows], own_sent_c.at[k], got_c.at[k], k, 0)
+
+    def send_own(source, place, send_sem, receive):
+        send(source, place, send_sem.at[0], receive.at[s], s + 2, h, has_right)
+        send(source, place, send_sem.at[1], receive.at[s], s - 2, h, has_left)
+        send(source, place, send_sem.at[2], receive.at[s], partner, h)
+
+    send_own(tokens_ref.at[:, columns_of(h)], tokens.at[h, own_rows], own_sent, got)
     local = [pltpu.make_async_copy(tokens_ref.at[:, columns_of(q)], tokens.at[q, own_rows],
                                    local_sem.at[q]) for q in range(parts)]
     local.append(pltpu.make_async_copy(cotangent_ref, cotangent.at[own_rows],
@@ -253,15 +288,24 @@
                            preferred_element_type=jnp.float32)
         return acc
 
-    def project(k):
-        rows = rows_of(flip(s, k))
-        if k:
-            place = tokens.at[flip(h, 1), rows]
-            remote(place, place, own_sent.at[0], pair_got.at[k], 0, 1).wait_recv()
-            place = tokens.at[flip(h, 3), rows]
-            remote(place, place, own_sent.at[0], relay_got.at[k], 0, 1).wait_recv()
+    def index_of(kind, j):
+        if kind == "own":
+            return s
+        if kind == "pair":
+            return partner
+        return line_block(j) * 2 + (side if kind == "line" else 1 - side)
+
+    def wait_for(place, semaphore):
+        remote(place, place, own_sent.at[2], semaphore, partner, h).wait_recv()
+
+    def project(kind, j=0):
+        index = index_of(kind, j)
+        rows = rows_of(index)
+        if kind != "own":
+            wait_for(tokens.at[flip(h, 1), rows], pair_got.at[index])
+            wait_for(tokens.at[flip(h, 3), rows], relay_got.at[index])
         acc = token_rows(rows, projection, slice(None))
-        if k == 0:
+        if kind == "own":
             base_q[...] = acc[:, :QW]
         base_kv[rows, :] = acc[:, QW:]
         half = acc.astype(jnp.bfloat16)
@@ -270,48 +314,68 @@
         key_t[:, rows] = half_f[:, QW : QW + D].T.astype(jnp.bfloat16)
         value_t[:, rows] = half_f[:, QW + D :].T.astype(jnp.bfloat16)
 
-    def arrived(k):
-        place = tokens.at[h, rows_of(flip(s, k))]
-        remote(place, place, own_sent.at[0], got.at[k], 1, 0).wait_recv()
-        if k % 2 == 0:
-            send(place, place, fold_sent.at[k], got.at[k + 1], 1, 0)
-        send(place, place, across_sent.at[k], across_got.at[k], 0, 2)
-        send(place, place, pair_sent.at[k], pair_got.at[k], 0, 1)
-
-    def arrived_c(k):
-        place = cotangent.at[rows_of(flip(s, k))]
-        remote(place, place, own_sent.at[0], got_c.at[k], 1, 0).wait_recv()
-        if k % 2 == 0:
-            send(place, place, fold_sent_c.at[k], got_c.at[k + 1], 1, 0)
-
-    def relay(k):
-        place = tokens.at[flip(h, 2), rows_of(flip(s, k))]
-        remote(place, place, own_sent.at[0], across_got.at[k], 0, 2).wait_recv()
-        send(place, place, relay_sent.at[k], relay_got.at[k], 0, 1)
+    def pass_on(place, index, line, fold, receive):
+        ahead = index // 2 < place_on_line
+        to_s = jnp.where(ahead, s + 2, s - 2)
+        more = jnp.where(ahead, place_on_line < length_of_line - 1, place_on_line > 0)
+        send(place, place, line.at[index], receive.at[index], to_s, h, more)
+        send(place, place, fold.at[index], receive.at[index], partner, h)
+
+    def arrived(kind, j=0):
+        index = index_of(kind, j)
+        place = tokens.at[h, rows_of(index)]
+        wait_for(place, got.at[index])
+        if kind == "line":
+            pass_on(place, index, line_sent, fold_sent, got)
+        send(place, place, across_sent.at[index], across_got.at[index], s, flip(h, 2))
+        send(place, place, pair_sent.at[index], pair_got.at[index], s, flip(h, 1))
+
+    def arrived_c(kind, j=0):
+        index = index_of(kind, j)
+        place = cotangent.at[rows_of(index)]
+        wait_for(place, got_c.at[index])
+        if kind == "line":
+            pass_on(place, index, line_sent_c, fold_sent_c, got_c)
+
+    def relay(kind, j=0):
+        index = index_of(kind, j)
+        place = tokens.at[flip(h, 2), rows_of(index)]
+        wait_for(place, across_got.at[index])
+        send(place, place, relay_sent.at[index], relay_got.at[index], s, flip(h, 1))
 
     for copy in local:
         copy.wait()
-    load.wait()
-
-    order = [even[0], 1] + [k for j in even[1:] for k in (j, )] + [k + 1 for k in even]
-    project_queue = [0] + order
-    for position, k in enumerate(order):
-        arrived(k)
-        if position >= 1:
-            relay(order[position - 1])
-        if position == 1:
-            project(project_queue.pop(0))
-        if position >= 4:
-            project(project_queue.pop(0))
-    relay(order[-1])
-    for k in even:
-        arrived_c(k)
-        project(project_queue.pop(0))
-    while project_queue:
-        project(project_queue.pop(0))
-    for k in order:
-        if k % 2:
-            arrived_c(k)
+
+    steps = length_of_line - 1
+    order = [("line", 0), ("pair", 0)]
+    for j in range(1, steps):
+        order += [("line", j), ("fold", j - 1)]
+    order.append(("fold", steps - 1))
+    queue = [("own", 0)] + order
+    cotangents = [("line", j) for j in range(steps)]
+    for position, item in enumerate(order):
+        arrived(*item)
+        if item == ("line", 1):
+            send_own(cotangent_ref, cotangent.at[own_rows], own_sent_c, got_c)
+        if position == 3:
+            load.wait()
+        if position >= 3:
+            relay(*order[position - 3])
+            project(*queue.pop(0))
+        if position >= 5 and cotangents:
+            arrived_c(*cotangents.pop(0))
+    for item in order[-3:]:
+        if cotangents:
+            arrived_c(*cotangents.pop(0))
+        relay(*item)
+        project(*queue.pop(0))
+    while cotangents:
+        arrived_c(*cotangents.pop(0))
+    while queue:
+        project(*queue.pop(0))
+    arrived_c("pair")
+    for j in range(steps):
+        arrived_c("fold", j)
 
     key_sum[...] = jnp.zeros_like(key_sum)
     value_sum[...] = jnp.zeros_like(value_sum)
@@ -374,7 +438,7 @@
 
     move_q[...] = token_rows(own_rows, weight_half, slice(0, QW))
     for q in range(1, parts):
-        send(norms.at[0], norms.at[q], norm_sent.at[q], norm_got.at[q], 0, q)
+        send(norms.at[0], norms.at[q], norm_sent.at[q], norm_got.at[q], s, flip(h, q))
 
     @pl.loop(0, total // tile)
     def _(block):
@@ -382,7 +446,7 @@
         move_kv[rows, :] = token_rows(rows, weight_half, slice(QW, None))
 
     for q in range(1, parts):
-        remote(norms.at[q], norms.at[q], norm_sent.at[0], norm_got.at[q], 0, q).wait_recv()
+        remote(norms.at[q], norms.at[q], norm_sent.at[0], norm_got.at[q], s, flip(h, q)).wait_recv()
     square_sum = jnp.sum(jnp.sum(norms[...], axis=0), keepdims=True)
     inverse = 1.0 / jnp.sqrt(square_sum)
     direction[...] = own_grad[...] * (root * inverse)
@@ -406,8 +470,14 @@
         context_t = jnp.dot(new_value_t, weights.astype(jnp.bfloat16),
                             preferred_element_type=jnp.float32) / sums
         out[:, g * D : (g + 1) * D] = context_t.T.astype(jnp.bfloat16)
-    for copy in sent:
-        copy.wait_send()
+    for copy, when in sent:
+        if when is None:
+            copy.wait_send()
+        else:
+
+            @pl.when(when)
+            def _():
+                copy.wait_send()
 
 
 def resident_step(tokens, projection, cotangent):
@@ -448,7 +518,7 @@
             pltpu.SemaphoreType.DMA((parts + 1,)),
             pltpu.SemaphoreType.DMA,
         ]
-        + [pltpu.SemaphoreType.DMA((seq_size,))] * 12
+        + [pltpu.SemaphoreType.DMA((seq_size,))] * 14
         + [pltpu.SemaphoreType.DMA((parts,))] * 2,
         compiler_params=pltpu.CompilerParams(
             collective_id=0, has_side_effects=True, vmem_limit_bytes=VMEM_BUDGET
@@ -461,7 +531,7 @@
     total = local_rows * seq_size
     share = features // seq_size
     held = total * (2 * features + 2 * QW + 12 * columns + 24 * D) + 4 * features * columns
-    pairs = seq_size >= 4 and seq_size & (seq_size - 1) == 0 and head_size == 4
+    pairs = seq_size >= 8 and seq_size & (seq_size - 1) == 0 and head_size == 4
     aligned = share % 128 == 0 and (features // head_size) % share == 0 and local_rows % 128 == 0
     return pairs and aligned and held < VMEM_BUDGET // 2
 

time: 79 us -> 72.3 us (0.915)
  Pallas kernels: 74.6 us -> 67.9 us
    pallas_call x1, Pallas kernels: 74.6 us -> 67.9 us  [resident_step(): pl.pallas_call(functools.partial(resident_kernel, seq_size, radius, root)...]
where the time goes in v3:
time: 72.3 us; the launch traced here: 72.1 us
  Pallas kernels  67.9 us (94%)
  local copies, waits for them, and re-layouts  3.63 us (5%)
    pallas_call x1, Pallas kernels, resident_step(): pl.pallas_call(functools.partial(resident_kernel, seq_size, radius, root)...  67.9 us
    unnamed x2, local copies, waits for them, and re-layouts  3.63 us

profile of v3, /device:TPU:0, one launch (start us, length us, event | category | flops | bytes accessed | tf_op | source)
XLA Modules:
  0.0 72.1 jit_solution(4872183423304824824)
XLA Ops:
  0.6 67.9 %resident.1 = (bf16[128,512]{1,0:T(8,128)(2,1)}, f32[256,768]{1,0:T(8,128)}) custom-call(bf16[128,2048]{1,0:T(8,128)(2,1)} %tokens_ref.1, bf16[128,512]{1,0:T(8,128)(2,1)} %cotangent_ref.1, bf16[2048,768]{1,0:T(8,128)(2,1)} %projection_hbm.1), custom_call_target="tpu_custom_call" | custom-call | tf_op jit(solution)/shard_map/resident/pallas_call | solution.py:493
  68.5 1.6 %copy.7 = bf16[128,512]{1,0:T(8,128)(2,1)} copy(bf16[128,512]{1,0:T(8,128)(2,1)} %get-tuple-element.4) | data formatting | bytes 262144
  70.1 2.1 %copy.8 = f32[256,768]{1,0:T(8,128)} copy(f32[256,768]{1,0:T(8,128)} %get-tuple-element.5) | data formatting | bytes 1572864

commit v4 on v3

--- a/solution.py
+++ b/solution.py
@@ -191,7 +191,7 @@
 
 def resident_kernel(
     seq_size, radius, root, tokens_ref, cotangent_ref, projection_hbm, out, direction,
-    tokens, cotangent, projection, projected, base_q, base_kv, key_t, value_t, grads,
+    tokens, cotangent, projection, projected, base_q, base_kv, key_t, grads,
     key_sum, value_sum, weight_half, own_grad, move_q, move_kv, norms,
     local_sem, load_sem, own_sent, own_sent_c, line_sent, line_sent_c, fold_sent, fold_sent_c,
     got, got_c, across_sent, pair_sent, relay_sent, across_got, pair_got, relay_got,
@@ -267,12 +267,16 @@
 
     own_rows = rows_of(s)
 
-    def send_own(source, place, send_sem, receive):
+    own_tokens = (tokens_ref.at[:, columns_of(h)], tokens.at[h, own_rows])
+    own_cotangent = (cotangent_ref, cotangent.at[own_rows])
+
+    def send_line(source, place, send_sem, receive):
         send(source, place, send_sem.at[0], receive.at[s], s + 2, h, has_right)
         send(source, place, send_sem.at[1], receive.at[s], s - 2, h, has_left)
-        send(source, place, send_sem.at[2], receive.at[s], partner, h)
-
-    send_own(tokens_ref.at[:, columns_of(h)], tokens.at[h, own_rows], own_sent, got)
+
+    send_line(*own_tokens, own_sent, got)
+    send(*own_tokens, own_sent.at[2], got.at[s], partner, h)
+    send(*own_cotangent, own_sent_c.at[2], got_c.at[s], partner, h)
     local = [pltpu.make_async_copy(tokens_ref.at[:, columns_of(q)], tokens.at[q, own_rows],
                                    local_sem.at[q]) for q in range(parts)]
     local.append(pltpu.make_async_copy(cotangent_ref, cotangent.at[own_rows],
@@ -312,7 +316,6 @@
         projected[rows, :] = half
         half_f = half.astype(jnp.float32)
         key_t[:, rows] = half_f[:, QW : QW + D].T.astype(jnp.bfloat16)
-        value_t[:, rows] = half_f[:, QW + D :].T.astype(jnp.bfloat16)
 
     def pass_on(place, index, line, fold, receive):
         ahead = index // 2 < place_on_line
@@ -355,14 +358,14 @@
     cotangents = [("line", j) for j in range(steps)]
     for position, item in enumerate(order):
         arrived(*item)
-        if item == ("line", 1):
-            send_own(cotangent_ref, cotangent.at[own_rows], own_sent_c, got_c)
+        if item == ("line", 0):
+            send_line(*own_cotangent, own_sent_c, got_c)
         if position == 3:
             load.wait()
         if position >= 3:
             relay(*order[position - 3])
             project(*queue.pop(0))
-        if position >= 5 and cotangents:
+        if position >= 4 and position % 2 == 0 and cotangents:
             arrived_c(*cotangents.pop(0))
     for item in order[-3:]:
         if cotangents:
@@ -387,7 +390,7 @@
         length = (block + 1) * tile
         rows = slice(block * tile, length)
 
-        @pl.loop(0, QUERY_PER_GROUP)
+        @pl.loop(0, QUERY_PER_GROUP, unroll=2)
         def _(head):
             columns = pl.ds(pl.multiple_of(head * D, D), D)
             query = projected[rows, columns]
@@ -400,13 +403,11 @@
             weights = jnp.exp2(scores * SCALE_LOG2 - top * SCALE_LOG2)
             probs = weights * (1.0 / jnp.sum(weights, axis=0, keepdims=True))
             probs_half = probs.astype(jnp.bfloat16)
-            context_t = jnp.dot(value_t[:, :length], probs_half,
-                                preferred_element_type=jnp.float32)
-            context_t = context_t.astype(jnp.bfloat16).astype(jnp.float32)
-            delta = jnp.sum(out_grad.astype(jnp.float32).T * context_t, axis=0, keepdims=True)
             prob_grad = lax.dot_general(projected[:length, QW + D :], out_grad, CONTRACT_LAST,
                                         preferred_element_type=jnp.float32)
-            score_grad = (probs * (prob_grad - delta)).astype(jnp.bfloat16)
+            weighted = probs * prob_grad
+            delta = jnp.sum(weighted, axis=0, keepdims=True)
+            score_grad = (weighted - probs * delta).astype(jnp.bfloat16)
             query_t = jnp.dot(key_t[:, :length], score_grad, preferred_element_type=jnp.float32)
             grads[rows, columns] = (query_t * SCALE).T.astype(jnp.bfloat16)
             key_sum[:length, :] += jnp.dot(score_grad, query, preferred_element_type=jnp.float32)
@@ -506,7 +507,6 @@
             pltpu.VMEM((local_rows, QW), f32),
             pltpu.VMEM((total, 2 * D), f32),
             pltpu.VMEM((D, total), bf16),
-            pltpu.VMEM((D, total), bf16),
             pltpu.VMEM((total, columns), bf16),
             pltpu.VMEM((total, D), f32),
             pltpu.VMEM((total, D), f32),

time: 72.3 us -> 67.1 us (0.928)
  Pallas kernels: 67.9 us -> 62.6 us
    pallas_call x1, Pallas kernels: 67.9 us -> 62.6 us  [resident_step(): pl.pallas_call(functools.partial(resident_kernel, seq_size, radius, root)...]
where the time goes in v4:
time: 67.1 us; the launch traced here: 66.9 us
  Pallas kernels  62.6 us (93%)
  local copies, waits for them, and re-layouts  3.63 us (5%)
    pallas_call x1, Pallas kernels, resident_step(): pl.pallas_call(functools.partial(resident_kernel, seq_size, radius, root)...  62.6 us
    unnamed x2, local copies, waits for them, and re-layouts  3.63 us

profile of v4, /device:TPU:0, one launch (start us, length us, event | category | flops | bytes accessed | tf_op | source)
XLA Modules:
  0.0 66.9 jit_solution(5955399134503790121)
XLA Ops:
  0.6 62.6 %resident.1 = (bf16[128,512]{1,0:T(8,128)(2,1)}, f32[256,768]{1,0:T(8,128)}) custom-call(bf16[128,2048]{1,0:T(8,128)(2,1)} %tokens_ref.1, bf16[128,512]{1,0:T(8,128)(2,1)} %cotangent_ref.1, bf16[2048,768]{1,0:T(8,128)(2,1)} %projection_hbm.1), custom_call_target="tpu_custom_call" | custom-call | tf_op jit(solution)/shard_map/resident/pallas_call | solution.py:494
  63.2 1.6 %copy.7 = bf16[128,512]{1,0:T(8,128)(2,1)} copy(bf16[128,512]{1,0:T(8,128)(2,1)} %get-tuple-element.4) | data formatting | bytes 262144
  64.8 2.1 %copy.8 = f32[256,768]{1,0:T(8,128)} copy(f32[256,768]{1,0:T(8,128)} %get-tuple-element.5) | data formatting | bytes 1572864

commit v5 on v4

--- a/solution.py
+++ b/solution.py
@@ -390,7 +390,7 @@
         length = (block + 1) * tile
         rows = slice(block * tile, length)
 
-        @pl.loop(0, QUERY_PER_GROUP, unroll=2)
+        @pl.loop(0, QUERY_PER_GROUP, unroll=4)
         def _(head):
             columns = pl.ds(pl.multiple_of(head * D, D), D)
             query = projected[rows, columns]
@@ -420,7 +420,7 @@
     per_part = width // share
     norms[0] = jnp.zeros_like(norms[0])
 
-    @pl.loop(0, parts * per_part)
+    @pl.loop(0, parts * per_part, unroll=2)
     def _(chunk):
         columns = pl.ds(pl.multiple_of((chunk % per_part) * share, share), share)
         rows = pl.ds(pl.multiple_of(chunk * share, share), share)

time: 67.1 us -> 65.7 us (0.979)
  Pallas kernels: 62.6 us -> 61.2 us
    pallas_call x1, Pallas kernels: 62.6 us -> 61.2 us  [resident_step(): pl.pallas_call(functools.partial(resident_kernel, seq_size, radius, root)...]
where the time goes in v5:
time: 65.7 us; the launch traced here: 65.5 us
  Pallas kernels  61.2 us (93%)
  local copies, waits for them, and re-layouts  3.63 us (6%)
    pallas_call x1, Pallas kernels, resident_step(): pl.pallas_call(functools.partial(resident_kernel, seq_size, radius, root)...  61.2 us
    unnamed x2, local copies, waits for them, and re-layouts  3.63 us

profile of v5, /device:TPU:0, one launch (start us, length us, event | category | flops | bytes accessed | tf_op | source)
XLA Modules:
  0.0 65.5 jit_solution(13276187946841719122)
XLA Ops:
  0.6 61.2 %resident.1 = (bf16[128,512]{1,0:T(8,128)(2,1)}, f32[256,768]{1,0:T(8,128)}) custom-call(bf16[128,2048]{1,0:T(8,128)(2,1)} %tokens_ref.1, bf16[128,512]{1,0:T(8,128)(2,1)} %cotangent_ref.1, bf16[2048,768]{1,0:T(8,128)(2,1)} %projection_hbm.1), custom_call_target="tpu_custom_call" | custom-call | tf_op jit(solution)/shard_map/resident/pallas_call | solution.py:494
  61.8 1.6 %copy.7 = bf16[128,512]{1,0:T(8,128)(2,1)} copy(bf16[128,512]{1,0:T(8,128)(2,1)} %get-tuple-element.4) | data formatting | bytes 262144
  63.4 2.1 %copy.8 = f32[256,768]{1,0:T(8,128)} copy(f32[256,768]{1,0:T(8,128)} %get-tuple-element.5) | data formatting | bytes 1572864
